TPU v7x, 32 devices: a whole 2x2x4 slice. The times are simulated.
32 devices in a mesh: group: 2 (over y), gx: 4 (over z), gy: 4 (over x, core).
Axes of the slice: x: 2, y: 2, z: 4, core: 2. Of those that a mesh axis runs over, the one named last changes fastest.
Arguments:
- displacement: float32 [2, 3, 32, 64, 128], P('group', None, 'gx', 'gy'), may hold values from -6 to 6
- velocity: float32 [2, 3, 32, 64, 128], P('group', None, 'gx', 'gy'), may hold values from -6 to 6
- modulus: float32 [2, 32, 64, 128], P('group', 'gx', 'gy'), may hold values from 1 to 4
- bond_words: int32 [2, 32, 64, 128], P(None, 'gx', 'gy'), may hold values from 0 to 2147483647, as said below
- coupling_map: int32 [3, 32, 64], P(None, 'gx', 'gy'), may hold values from 0 to 2
Outputs:
- new_displacement: float32 [2, 3, 32, 64, 128], P('group', None, 'gx', 'gy')
- new_velocity: float32 [2, 3, 32, 64, 128], P('group', None, 'gx', 'gy')
Inputs may be any that keep to these rules, and one draw needn't show every extreme that they name: `bond_words`: bonds to positions outside the zone are 0; bit 30 of word 1 is 0.
All inputs are finite; a program needn't handle non-finite values.
Results may differ from a plain program's by a relative error of at most 0.0001.
Values sent between devices are 32-bit elements; how exact they have to be, the bound alone decides.
A program may use at most 64 MiB of HBM per device.

v0:
```python
import math

import jax
import jax.numpy as jnp
import numpy as np
from jax import lax
from jax.sharding import PartitionSpec as P

time_step = 0.1
bond_scale = 1.0


def with_halo(block, sides, width):
    for axis, dim in sides:
        count = lax.axis_size(axis)
        forward = [(i, i + 1) for i in range(count - 1)]
        backward = [(target, source) for source, target in forward]
        low = lax.ppermute(
            lax.slice_in_dim(block, block.shape[dim] - width, None, axis=dim), axis, forward
        )
        high = lax.ppermute(lax.slice_in_dim(block, 0, width, axis=dim), axis, backward)
        block = jnp.concatenate([low, block, high], axis=dim)
    return block


def passed_along(block, axis, distance):
    devices = range(lax.axis_size(axis))
    route = [(i - distance, i) for i in devices if i - distance in devices]
    return lax.ppermute(block, axis, route)


def half_offsets():
    table = []
    for delta_x in range(-3, 4):
        for delta_y in range(-3, 4):
            for delta_z in range(-3, 4):
                radius = delta_x * delta_x + delta_y * delta_y + delta_z * delta_z
                if 0 < radius <= 9 and (delta_x, delta_y, delta_z) > (0, 0, 0):
                    table.append((delta_x, delta_y, delta_z))
    return table


def hex_stiffness():
    poisson = 0.3
    lame_first = poisson / ((1.0 + poisson) * (1.0 - 2.0 * poisson))
    shear_modulus = 0.5 / (1.0 + poisson)
    elastic = np.zeros((6, 6))
    elastic[:3, :3] = lame_first
    for axis_id in range(3):
        elastic[axis_id, axis_id] += 2.0 * shear_modulus
        elastic[3 + axis_id, 3 + axis_id] = shear_modulus
    points = [0.5 - 0.5 / math.sqrt(3.0), 0.5 + 0.5 / math.sqrt(3.0)]
    result = np.zeros((24, 24))
    shear_pairs = ((0, 1), (1, 2), (0, 2))
    for along_x in points:
        for along_y in points:
            for along_z in points:
                coords = (along_x, along_y, along_z)
                gradients = np.zeros((3, 8))
                for corner in range(8):
                    corner_bits = (corner >> 2 & 1, corner >> 1 & 1, corner & 1)
                    factors = [
                        coords[axis_id] if corner_bits[axis_id] else 1.0 - coords[axis_id]
                        for axis_id in range(3)
                    ]
                    slopes = [1.0 if corner_bits[axis_id] else -1.0 for axis_id in range(3)]
                    gradients[0, corner] = slopes[0] * factors[1] * factors[2]
                    gradients[1, corner] = factors[0] * slopes[1] * factors[2]
                    gradients[2, corner] = factors[0] * factors[1] * slopes[2]
                strain = np.zeros((6, 24))
                for axis_id in range(3):
                    strain[axis_id, axis_id * 8 : axis_id * 8 + 8] = gradients[axis_id]
                for shear_row, pair in enumerate(shear_pairs):
                    left_axis, right_axis = pair
                    strain[3 + shear_row, left_axis * 8 : left_axis * 8 + 8] = gradients[right_axis]
                    strain[3 + shear_row, right_axis * 8 : right_axis * 8 + 8] = gradients[
                        left_axis
                    ]
                result += strain.T @ elastic @ strain / 8.0
    return result


def bond_sum(field_pad, words_pad, modulus_pad, size_x, size_y, size_z):

    def window(array, delta_x, delta_y, delta_z):
        return array[
            ...,
            3 + delta_x : 3 + delta_x + size_x,
            3 + delta_y : 3 + delta_y + size_y,
            3 + delta_z : 3 + delta_z + size_z,
        ]

    centre = window(field_pad, 0, 0, 0)
    centre_modulus = window(modulus_pad, 0, 0, 0)
    centre_words = window(words_pad, 0, 0, 0)
    summed = jnp.zeros_like(centre)
    for number, offset in enumerate(half_offsets()):
        delta_x, delta_y, delta_z = offset
        word_id = number // 31
        bit_id = number % 31
        factor = (
            0.5
            * bond_scale
            / float(delta_x * delta_x + delta_y * delta_y + delta_z * delta_z) ** 1.5
        )
        ahead_diff = window(field_pad, delta_x, delta_y, delta_z) - centre
        behind_diff = window(field_pad, -delta_x, -delta_y, -delta_z) - centre
        ahead_proj = delta_x * ahead_diff[0] + delta_y * ahead_diff[1] + delta_z * ahead_diff[2]
        behind_proj = delta_x * behind_diff[0] + delta_y * behind_diff[1] + delta_z * behind_diff[2]
        ahead_flag = (centre_words[word_id] >> bit_id & 1).astype(jnp.float32)
        behind_flag = (
            window(words_pad[word_id], -delta_x, -delta_y, -delta_z) >> bit_id & 1
        ).astype(jnp.float32)
        strength = (
            ahead_flag
            * (centre_modulus + window(modulus_pad, delta_x, delta_y, delta_z))
            * ahead_proj
        )
        strength = (
            strength
            + behind_flag
            * (centre_modulus + window(modulus_pad, -delta_x, -delta_y, -delta_z))
            * behind_proj
        )
        strength = factor * strength
        summed = summed + jnp.stack([delta_x * strength, delta_y * strength, delta_z * strength])
    return summed


def couple(below_top, map_layers):
    coupled = jnp.zeros_like(below_top)
    for layer_id in range(below_top.shape[3]):
        coupled = coupled + jnp.where(
            map_layers[None] == layer_id, below_top[..., layer_id : layer_id + 1], 0.0
        )
    return coupled


def spread(reaction, map_layers):
    columns = []
    for layer_id in range(reaction.shape[3]):
        columns.append(jnp.sum(jnp.where(map_layers[None] == layer_id, reaction, 0.0), axis=3))
    return jnp.stack(columns, axis=3)


def slab_forces(extended, modulus_rim, start_x, start_y, full_x, full_y, rows_x, rows_y, depth_z):
    stiffness = jnp.asarray(hex_stiffness(), dtype=jnp.float32)
    field_pad = jnp.pad(extended, ((0, 0), (0, 0), (0, 0), (0, 1)))
    pieces = []
    for component in range(3):
        for corner in range(8):
            corner_x, corner_y, corner_z = (corner >> 2 & 1, corner >> 1 & 1, corner & 1)
            pieces.append(
                field_pad[
                    component,
                    2 + corner_x : 3 + corner_x + rows_x,
                    2 + corner_y : 3 + corner_y + rows_y,
                    corner_z : corner_z + depth_z,
                ]
            )
    gathered = jnp.stack(pieces).reshape(24, -1)
    global_x = start_x - 1 + jnp.arange(rows_x + 1)
    global_y = start_y - 1 + jnp.arange(rows_y + 1)
    inside = (
        ((global_x >= 0) & (global_x < full_x - 1))[:, None, None]
        & ((global_y >= 0) & (global_y < full_y - 1))[None, :, None]
        & (jnp.arange(depth_z) < depth_z - 1)[None, None, :]
    ).astype(jnp.float32)
    element_modulus = modulus_rim[2 : 3 + rows_x, 2 : 3 + rows_y, :] * inside
    result = jnp.dot(
        stiffness, gathered, precision=lax.Precision.HIGHEST, preferred_element_type=jnp.float32
    )
    result = result.reshape(24, rows_x + 1, rows_y + 1, depth_z) * element_modulus[None]
    result_pad = jnp.pad(result, ((0, 0), (0, 0), (0, 0), (1, 0)))
    forces = []
    for component in range(3):
        summed = jnp.zeros((rows_x, rows_y, depth_z), jnp.float32)
        for corner in range(8):
            corner_x, corner_y, corner_z = (corner >> 2 & 1, corner >> 1 & 1, corner & 1)
            summed = (
                summed
                - result_pad[
                    component * 8 + corner,
                    1 - corner_x : 1 - corner_x + rows_x,
                    1 - corner_y : 1 - corner_y + rows_y,
                    1 - corner_z : 1 - corner_z + depth_z,
                ]
            )
        forces.append(summed)
    return jnp.stack(forces)


def per_device(displacement, velocity, modulus, bond_words, coupling_map):
    rows_x, rows_y, depth_z = (displacement.shape[2], displacement.shape[3], displacement.shape[4])
    layers = coupling_map.shape[0]
    full_x = rows_x * lax.axis_size("gx")
    full_y = rows_y * lax.axis_size("gy")
    start_x = lax.axis_index("gx") * rows_x
    start_y = lax.axis_index("gy") * rows_y
    is_zone = lax.axis_index("group") == 0
    words_rim = with_halo(bond_words, (("gx", 1), ("gy", 2)), 3)
    modulus_rim = with_halo(modulus[0], (("gx", 0), ("gy", 1)), 3)
    map_layers = jnp.transpose(coupling_map, (1, 2, 0))
    z_padding = ((0, 0), (0, 0), (0, 0), (3, 3))
    words_pad = jnp.pad(words_rim, z_padding)
    modulus_pad = jnp.pad(modulus_rim, ((0, 0), (0, 0), (3, 3)))
    layer_ids = jnp.arange(depth_z)
    moving = (layer_ids >= layers)[None, None, None, :]
    unclamped = (layer_ids > 0)[None, None, None, :]
    position_x = start_x + jnp.arange(rows_x)
    position_y = start_y + jnp.arange(rows_y)
    count_x = (position_x > 0).astype(jnp.float32) + (position_x < full_x - 1).astype(jnp.float32)
    count_y = (position_y > 0).astype(jnp.float32) + (position_y < full_y - 1).astype(jnp.float32)
    count_z = (layer_ids > 0).astype(jnp.float32) + (layer_ids < depth_z - 1).astype(jnp.float32)
    lumped_mass = count_x[:, None, None] * count_y[None, :, None] * count_z[None, None, :] / 8.0
    current = displacement[0]
    velocity_now = velocity[0]
    below_top = passed_along(current[:, :, :, depth_z - layers :], "group", -1)
    coupled = couple(below_top, map_layers)
    current = jnp.where(
        is_zone, jnp.concatenate([coupled, current[:, :, :, layers:]], axis=3), current
    )
    extended = with_halo(current, (("gx", 1), ("gy", 2)), 3)

    def zone_branch():
        return bond_sum(
            jnp.pad(extended, z_padding), words_pad, modulus_pad, rows_x, rows_y, depth_z
        )

    def slab_branch():
        return slab_forces(
            extended, modulus_rim, start_x, start_y, full_x, full_y, rows_x, rows_y, depth_z
        )

    forces = lax.cond(is_zone, zone_branch, slab_branch)
    reaction = passed_along(forces[:, :, :, :layers], "group", 1)
    interface = jnp.pad(
        spread(reaction, map_layers), ((0, 0), (0, 0), (0, 0), (depth_z - layers, 0))
    )
    slab_total = forces + interface
    zone_velocity = jnp.where(moving, velocity_now + time_step * forces, velocity_now)
    zone_field = jnp.where(moving, current + time_step * zone_velocity, current)
    slab_velocity = jnp.where(unclamped, velocity_now + time_step * slab_total / lumped_mass, 0.0)
    slab_field = jnp.where(unclamped, current + time_step * slab_velocity, 0.0)
    velocity_now = jnp.where(is_zone, zone_velocity, slab_velocity)
    current = jnp.where(is_zone, zone_field, slab_field)
    return (current[None], velocity_now[None])


def solution(mesh):
    return jax.shard_map(
        per_device,
        mesh=mesh,
        in_specs=(
            P("group", None, "gx", "gy", None),
            P("group", None, "gx", "gy", None),
            P("group", "gx", "gy", None),
            P(None, "gx", "gy", None),
            P(None, "gx", "gy"),
        ),
        out_specs=(P("group", None, "gx", "gy", None), P("group", None, "gx", "gy", None)),
        check_vma=False,
    )
```

profile of v0, /device:TPU:14, one launch (start us, length us, event | category | flops | bytes accessed | tf_op | source)
XLA Modules:
  0.0 111.2 jit_solution(14668985967839239212)
XLA Ops:
  2.2 2.4 %collective-permute-start = (f32[3,8,16,3]{2,1,0,3:T(8,128)S(1)}, f32[3,8,16,3]{2,1,0,3:T(8,128)S(1)}, u32[]{:S(2)}, u32[]{:S(2)}) collective-permute-start(f32[3,8,16,3]{2,1,0,3:T(8,128)S(1)} %slice.2951), channel_id=1, source_target_pairs={{16,0},{17,1},{18,2},{19,3},{20,4},{21,5},{22,6},{23,7},{24,8},{25... | collective-permute-start | bytes 13832 | tf_op jit(solution)/shard_map/ppermute | solution.py:29
  5.3 2.3 %collective-permute-start.6 = (f32[3,16,128]{2,1,0:T(8,128)S(1)}, f32[3,16,128]{2,1,0:T(8,128)S(1)}, u32[]{:S(2)}, u32[]{:S(2)}) collective-permute-start(f32[3,16,128]{2,1,0:T(8,128)S(1)} %get-tuple-element.425), channel_id=1, source_target_pairs={{4,0},{8,4},{12,8},{5,1},{9,5},{13,9},{6,2},{10,6},{14,10},{7,3},{... | collective-permute-start | bytes 73736 | tf_op jit(solution)/shard_map/ppermute | solution.py:21
  7.7 3.5 %collective-permute-start.5 = (f32[3,16,128]{2,1,0:T(8,128)S(1)}, f32[3,16,128]{2,1,0:T(8,128)S(1)}, u32[]{:S(2)}, u32[]{:S(2)}) collective-permute-start(f32[3,16,128]{2,1,0:T(8,128)S(1)} %get-tuple-element.424), channel_id=1, source_target_pairs={{0,4},{4,8},{8,12},{1,5},{5,9},{9,13},{2,6},{6,10},{10,14},{3,7},{... | collective-permute-start | bytes 73736 | tf_op jit(solution)/shard_map/ppermute | solution.py:18
  12.6 3.5 %collective-permute-start.9 = (s32[2,3,16,128]{3,2,1,0:T(8,128)S(1)}, s32[2,3,16,128]{3,2,1,0:T(8,128)}, u32[]{:S(2)}, u32[]{:S(2)}) collective-permute-start(s32[2,3,16,128]{3,2,1,0:T(8,128)S(1)} %get-tuple-element.421), channel_id=1, source_target_pairs={{0,4},{4,8},{8,12},{1,5},{5,9},{9,13},{2,6},{6,10},{10,14},{3,7},{... | collective-permute-start | bytes 147464 | tf_op jit(solution)/shard_map/ppermute | solution.py:18
  16.1 3.0 %collective-permute-start.10 = (s32[2,3,16,128]{3,2,1,0:T(8,128)}, s32[2,3,16,128]{3,2,1,0:T(8,128)}, u32[]{:S(2)}, u32[]{:S(2)}) collective-permute-start(s32[2,3,16,128]{3,2,1,0:T(8,128)} %get-tuple-element.420), channel_id=1, source_target_pairs={{4,0},{8,4},{12,8},{5,1},{9,5},{13,9},{6,2},{10,6},{14,10},{7,3},{... | collective-permute-start | bytes 147464 | tf_op jit(solution)/shard_map/ppermute | solution.py:21
  24.7 1.9 %collective-permute-start.8 = (f32[14,3,128]{2,1,0:T(4,128)S(1)}, f32[14,3,128]{2,1,0:T(4,128)S(1)}, u32[]{:S(2)}, u32[]{:S(2)}) collective-permute-start(f32[14,3,128]{2,1,0:T(4,128)S(1)} %get-tuple-element.423), channel_id=1, source_target_pairs={{1,0},{2,1},{3,2},{5,4},{6,5},{7,6},{9,8},{10,9},{11,10},{13,12},{... | collective-permute-start | bytes 64520 | tf_op jit(solution)/shard_map/ppermute | solution.py:21
  26.6 2.5 %collective-permute-start.7 = (f32[14,3,128]{2,1,0:T(4,128)S(1)}, f32[14,3,128]{2,1,0:T(4,128)S(1)}, u32[]{:S(2)}, u32[]{:S(2)}) collective-permute-start(f32[14,3,128]{2,1,0:T(4,128)S(1)} %get-tuple-element.422), channel_id=1, source_target_pairs={{0,1},{1,2},{2,3},{4,5},{5,6},{6,7},{8,9},{9,10},{10,11},{12,13},{... | collective-permute-start | bytes 64520 | tf_op jit(solution)/shard_map/ppermute | solution.py:18
  29.1 2.2 %fusion.1075 = (f32[3,3,16,128]{2,1,0,3:T(4,128)S(1)}, f32[3,3,16,128]{2,1,0,3:T(4,128)S(1)}) fusion(f32[3,8,16,128]{2,1,0,3:T(8,128)} %maximum_select_fusion), kind=kLoop, calls=%fused_computation.1850 | loop fusion | bytes 294912 | tf_op jit(solution)/shard_map/slice | solution.py:19
  31.6 1.9 %collective-permute-start.2 = (f32[3,3,16,128]{3,2,1,0:T(8,128)S(1)}, f32[3,3,16,128]{3,2,1,0:T(8,128)S(1)}, u32[]{:S(2)}, u32[]{:S(2)}) collective-permute-start(f32[3,3,16,128]{3,2,1,0:T(8,128)S(1)} %copy.45), channel_id=1, source_target_pairs={{4,0},{8,4},{12,8},{5,1},{9,5},{13,9},{6,2},{10,6},{14,10},{7,3},{... | collective-permute-start | bytes 221192 | tf_op jit(solution)/shard_map/ppermute | solution.py:21
  33.8 3.9 %collective-permute-start.1 = (f32[3,3,16,128]{3,2,1,0:T(8,128)S(1)}, f32[3,3,16,128]{3,2,1,0:T(8,128)S(1)}, u32[]{:S(2)}, u32[]{:S(2)}) collective-permute-start(f32[3,3,16,128]{3,2,1,0:T(8,128)S(1)} %copy.44), channel_id=1, source_target_pairs={{0,4},{4,8},{8,12},{1,5},{5,9},{9,13},{2,6},{6,10},{10,14},{3,7},{... | collective-permute-start | bytes 221192 | tf_op jit(solution)/shard_map/ppermute | solution.py:18
  40.1 2.6 %collective-permute-start.12 = (s32[2,14,3,128]{3,2,1,0:T(4,128)}, s32[2,14,3,128]{3,2,1,0:T(4,128)}, u32[]{:S(2)}, u32[]{:S(2)}) collective-permute-start(s32[2,14,3,128]{3,2,1,0:T(4,128)} %get-tuple-element.419), channel_id=1, source_target_pairs={{1,0},{2,1},{3,2},{5,4},{6,5},{7,6},{9,8},{10,9},{11,10},{13,12},{... | collective-permute-start | bytes 129032 | tf_op jit(solution)/shard_map/ppermute | solution.py:21
  42.7 2.3 %collective-permute-start.11 = (s32[2,14,3,128]{3,2,1,0:T(4,128)}, s32[2,14,3,128]{3,2,1,0:T(4,128)}, u32[]{:S(2)}, u32[]{:S(2)}) collective-permute-start(s32[2,14,3,128]{3,2,1,0:T(4,128)} %get-tuple-element.418), channel_id=1, source_target_pairs={{0,1},{1,2},{2,3},{4,5},{5,6},{6,7},{8,9},{9,10},{10,11},{12,13},{... | collective-permute-start | bytes 129032 | tf_op jit(solution)/shard_map/ppermute | solution.py:18
  47.4 2.6 %pad_maximum_fusion.1 = f32[3,14,16,128]{2,1,0,3:T(8,128)S(1)} fusion(f32[3,3,16,128]{2,1,0,3:T(4,128)} %copy.47, f32[3,8,16,128]{2,1,0,3:T(8,128)} %maximum_select_fusion, f32[3,3,16,128]{2,1,0,3:T(4,128)} %copy.46), kind=kLoop, calls=%fused_computation.1800 | loop fusion | flops 172032 | bytes 688128 | tf_op jit(solution)/shard_map/concatenate | solution.py:22
  49.9 3.6 %fusion.1074 = (f32[3,14,3,128]{2,1,0,3:T(8,128)}, f32[3,14,3,128]{2,1,0,3:T(8,128)}) fusion(f32[3,14,16,128]{2,1,0,3:T(8,128)S(1)} %pad_maximum_fusion.1), kind=kLoop, calls=%fused_computation.1849 | loop fusion | bytes 258048 | tf_op jit(solution)/shard_map/slice | solution.py:19
  55.3 3.1 %copy.49 = f32[3,14,3,128]{3,1,2,0:T(8,128)} copy(f32[3,14,3,128]{2,1,0,3:T(8,128)} %get-tuple-element.415) | data formatting | bytes 129024 | tf_op jit(solution)/shard_map/slice | solution.py:21
  58.5 3.2 %collective-permute-start.4 = (f32[3,14,3,128]{3,1,2,0:T(8,128)}, f32[3,14,3,128]{3,1,2,0:T(8,128)}, u32[]{:S(2)}, u32[]{:S(2)}) collective-permute-start(f32[3,14,3,128]{3,1,2,0:T(8,128)} %copy.49), channel_id=1, source_target_pairs={{1,0},{2,1},{3,2},{5,4},{6,5},{7,6},{9,8},{10,9},{11,10},{13,12},{... | collective-permute-start | bytes 193544 | tf_op jit(solution)/shard_map/ppermute | solution.py:21
  63.5 1.9 %collective-permute-start.3 = (f32[3,14,3,128]{3,1,2,0:T(8,128)}, f32[3,14,3,128]{3,1,2,0:T(8,128)S(1)}, u32[]{:S(2)}, u32[]{:S(2)}) collective-permute-start(f32[3,14,3,128]{3,1,2,0:T(8,128)} %copy.48), channel_id=1, source_target_pairs={{0,1},{1,2},{2,3},{4,5},{5,6},{6,7},{8,9},{9,10},{10,11},{12,13},{... | collective-permute-start | bytes 193544 | tf_op jit(solution)/shard_map/ppermute | solution.py:18
  67.3 2.1 %collective-permute-done.3 = f32[3,14,3,128]{3,1,2,0:T(8,128)S(1)} collective-permute-done((f32[3,14,3,128]{3,1,2,0:T(8,128)}, f32[3,14,3,128]{3,1,2,0:T(8,128)S(1)}, u32[]{:S(2)}, u32[]{:S(2)}) %collective-permute-start.3) | collective-permute-done | bytes 64544 | tf_op jit(solution)/shard_map/ppermute | solution.py:18
  70.5 24.0 %conditional.1 = (f32[3,8,16,128]{3,2,1,0:T(8,128)S(1)}) conditional(s32[]{:T(128)} %convert_element_type.605, (f32[3,14,22,128]{3,2,1,0:T(8,128)S(1)}, s32[]{:T(128)}, s32[]{:T(128)}, f32[14,22,128]{2,1,0:T(8,128)S(1)}) %tuple.18, (s32[2,14,22,128]{3,2,1,0:T(8,128)S(1)}, f32[14,22,128]{2,1,0:T(8,128)S(1)}, ...), branch_computations={%region_0.1_spmd.clone, %region_1.2_spmd} | conditional | flops 136365696 | bytes 112835016 | solution.py:235
  87.2 1.8 %reshape.1197 = f32[24,19584]{1,0:T(8,128)S(1)} reshape(f32[24,9,17,128]{3,2,1,0:T(8,128)} %fusion.982) | data formatting | bytes 3760128 | tf_op jit(solution)/shard_map/cond/branch_0_fun/reshape | solution.py:161
  89.0 2.9 %fusion.1078 = f32[24,19584]{1,0:T(8,128)} fusion(f32[24,24]{1,0:T(8,128)S(1)} %copy-done.8, f32[24,19584]{1,0:T(8,128)S(1)} %reshape.1197), kind=kOutput, calls=%fused_computation.1853 | convolution fusion | flops 135364608 | bytes 3762432 | tf_op jit(solution)/shard_map/cond/branch_0_fun/dot_general | solution.py:170
  98.7 3.2 %collective-permute-done.13 = f32[3,8,16,3]{2,1,0,3:T(8,128)} collective-permute-done((f32[3,8,16,3]{2,1,0,3:T(8,128)}, f32[3,8,16,3]{2,1,0,3:T(8,128)}, u32[]{:S(2)}, u32[]{:S(2)}) %collective-permute-start.13) | collective-permute-done | bytes 4640 | tf_op jit(solution)/shard_map/ppermute | solution.py:29
  102.7 4.7 %select_bitcast_fusion = (f32[1,3,8,16,128]{3,2,1,4,0:T(8,128)}, f32[1,3,8,16,128]{3,2,1,4,0:T(8,128)}) fusion(pred[]{:T(512)S(6)} %eq.27, f32[3,8,16,128]{2,1,0,3:T(8,128)} %copy.54, f32[1,3,8,16,128]{3,2,1,4,0:T(8,128)S(1)} %copy-done.1, pred[128]{0:T(512)(128)(4,1)} %get-tuple-element.433, f32[8,16,128]{1,0,2:T(8,128)} %multiply_multiply_fusion, ...), kind=kLoop, calls=%fused_computation.1814 | loop fusion | flops 1032192 | bytes 1250049 | tf_op jit(solution)/shard_map/broadcast_in_dim | solution.py:247
  107.3 2.6 %copy.57 = f32[1,3,8,16,128]{4,3,2,1,0:T(8,128)} copy(f32[1,3,8,16,128]{3,2,1,4,0:T(8,128)} %get-tuple-element.413) | data formatting | bytes 393216
  (104 shorter events, 45.9 us)
Async XLA Ops:
  0.6 20.9 %copy-start.5 = (f32[1,3,8,16,128]{4,3,2,1,0:T(8,128)S(1)}, f32[1,3,8,16,128]{4,3,2,1,0:T(8,128)}, u32[]{:S(2)}) copy-start(f32[1,3,8,16,128]{4,3,2,1,0:T(8,128)} %param.9) | copy-start | bytes 589828
  2.2 21.1 %collective-permute-start = (f32[3,8,16,3]{2,1,0,3:T(8,128)S(1)}, f32[3,8,16,3]{2,1,0,3:T(8,128)S(1)}, u32[]{:S(2)}, u32[]{:S(2)}) collective-permute-start(f32[3,8,16,3]{2,1,0,3:T(8,128)S(1)} %slice.2951), channel_id=1, source_target_pairs={{16,0},{17,1},{18,2},{19,3},{20,4},{21,5},{22,6},{23,7},{24,8},{25... | collective-permute-start | bytes 13832 | tf_op jit(solution)/shard_map/ppermute | solution.py:29
  5.3 19.3 %collective-permute-start.6 = (f32[3,16,128]{2,1,0:T(8,128)S(1)}, f32[3,16,128]{2,1,0:T(8,128)S(1)}, u32[]{:S(2)}, u32[]{:S(2)}) collective-permute-start(f32[3,16,128]{2,1,0:T(8,128)S(1)} %get-tuple-element.425), channel_id=1, source_target_pairs={{4,0},{8,4},{12,8},{5,1},{9,5},{13,9},{6,2},{10,6},{14,10},{7,3},{... | collective-permute-start | bytes 73736 | tf_op jit(solution)/shard_map/ppermute | solution.py:21
  7.7 16.9 %collective-permute-start.5 = (f32[3,16,128]{2,1,0:T(8,128)S(1)}, f32[3,16,128]{2,1,0:T(8,128)S(1)}, u32[]{:S(2)}, u32[]{:S(2)}) collective-permute-start(f32[3,16,128]{2,1,0:T(8,128)S(1)} %get-tuple-element.424), channel_id=1, source_target_pairs={{0,4},{4,8},{8,12},{1,5},{5,9},{9,13},{2,6},{6,10},{10,14},{3,7},{... | collective-permute-start | bytes 73736 | tf_op jit(solution)/shard_map/ppermute | solution.py:18
  12.6 25.2 %collective-permute-start.9 = (s32[2,3,16,128]{3,2,1,0:T(8,128)S(1)}, s32[2,3,16,128]{3,2,1,0:T(8,128)}, u32[]{:S(2)}, u32[]{:S(2)}) collective-permute-start(s32[2,3,16,128]{3,2,1,0:T(8,128)S(1)} %get-tuple-element.421), channel_id=1, source_target_pairs={{0,4},{4,8},{8,12},{1,5},{5,9},{9,13},{2,6},{6,10},{10,14},{3,7},{... | collective-permute-start | bytes 147464 | tf_op jit(solution)/shard_map/ppermute | solution.py:18
  16.1 22.5 %collective-permute-start.10 = (s32[2,3,16,128]{3,2,1,0:T(8,128)}, s32[2,3,16,128]{3,2,1,0:T(8,128)}, u32[]{:S(2)}, u32[]{:S(2)}) collective-permute-start(s32[2,3,16,128]{3,2,1,0:T(8,128)} %get-tuple-element.420), channel_id=1, source_target_pairs={{4,0},{8,4},{12,8},{5,1},{9,5},{13,9},{6,2},{10,6},{14,10},{7,3},{... | collective-permute-start | bytes 147464 | tf_op jit(solution)/shard_map/ppermute | solution.py:21
  19.8 3.4 %copy-start.6 = (pred[8,16,3]{1,0,2:T(8,128)(4,1)}, pred[8,16,3]{1,0,2:T(8,128)(4,1)S(1)}, u32[]{:S(2)}) copy-start(pred[8,16,3]{1,0,2:T(8,128)(4,1)S(1)} %get-tuple-element.431) | copy-start | bytes 1156
  23.2 1.4 %copy-start.3 = (f32[1,8,16,128]{3,2,1,0:T(8,128)S(1)}, f32[1,8,16,128]{3,2,1,0:T(8,128)}, u32[]{:S(2)}) copy-start(f32[1,8,16,128]{3,2,1,0:T(8,128)} %param.10) | copy-start | bytes 196612
  24.7 9.2 %collective-permute-start.8 = (f32[14,3,128]{2,1,0:T(4,128)S(1)}, f32[14,3,128]{2,1,0:T(4,128)S(1)}, u32[]{:S(2)}, u32[]{:S(2)}) collective-permute-start(f32[14,3,128]{2,1,0:T(4,128)S(1)} %get-tuple-element.423), channel_id=1, source_target_pairs={{1,0},{2,1},{3,2},{5,4},{6,5},{7,6},{9,8},{10,9},{11,10},{13,12},{... | collective-permute-start | bytes 64520 | tf_op jit(solution)/shard_map/ppermute | solution.py:21
  26.6 12.0 %copy-start.4 = (s32[2,8,16,128]{3,2,1,0:T(8,128)S(1)}, s32[2,8,16,128]{3,2,1,0:T(8,128)}, u32[]{:S(2)}) copy-start(s32[2,8,16,128]{3,2,1,0:T(8,128)} %param.11) | copy-start | bytes 393220
  26.6 11.2 %collective-permute-start.7 = (f32[14,3,128]{2,1,0:T(4,128)S(1)}, f32[14,3,128]{2,1,0:T(4,128)S(1)}, u32[]{:S(2)}, u32[]{:S(2)}) collective-permute-start(f32[14,3,128]{2,1,0:T(4,128)S(1)} %get-tuple-element.422), channel_id=1, source_target_pairs={{0,1},{1,2},{2,3},{4,5},{5,6},{6,7},{8,9},{9,10},{10,11},{12,13},{... | collective-permute-start | bytes 64520 | tf_op jit(solution)/shard_map/ppermute | solution.py:18
  31.6 13.4 %collective-permute-start.2 = (f32[3,3,16,128]{3,2,1,0:T(8,128)S(1)}, f32[3,3,16,128]{3,2,1,0:T(8,128)S(1)}, u32[]{:S(2)}, u32[]{:S(2)}) collective-permute-start(f32[3,3,16,128]{3,2,1,0:T(8,128)S(1)} %copy.45), channel_id=1, source_target_pairs={{4,0},{8,4},{12,8},{5,1},{9,5},{13,9},{6,2},{10,6},{14,10},{7,3},{... | collective-permute-start | bytes 221192 | tf_op jit(solution)/shard_map/ppermute | solution.py:21
  33.8 12.4 %collective-permute-start.1 = (f32[3,3,16,128]{3,2,1,0:T(8,128)S(1)}, f32[3,3,16,128]{3,2,1,0:T(8,128)S(1)}, u32[]{:S(2)}, u32[]{:S(2)}) collective-permute-start(f32[3,3,16,128]{3,2,1,0:T(8,128)S(1)} %copy.44), channel_id=1, source_target_pairs={{0,4},{4,8},{8,12},{1,5},{5,9},{9,13},{2,6},{6,10},{10,14},{3,7},{... | collective-permute-start | bytes 221192 | tf_op jit(solution)/shard_map/ppermute | solution.py:18
  40.1 25.3 %collective-permute-start.12 = (s32[2,14,3,128]{3,2,1,0:T(4,128)}, s32[2,14,3,128]{3,2,1,0:T(4,128)}, u32[]{:S(2)}, u32[]{:S(2)}) collective-permute-start(s32[2,14,3,128]{3,2,1,0:T(4,128)} %get-tuple-element.419), channel_id=1, source_target_pairs={{1,0},{2,1},{3,2},{5,4},{6,5},{7,6},{9,8},{10,9},{11,10},{13,12},{... | collective-permute-start | bytes 129032 | tf_op jit(solution)/shard_map/ppermute | solution.py:21
  42.7 22.7 %collective-permute-start.11 = (s32[2,14,3,128]{3,2,1,0:T(4,128)}, s32[2,14,3,128]{3,2,1,0:T(4,128)}, u32[]{:S(2)}, u32[]{:S(2)}) collective-permute-start(s32[2,14,3,128]{3,2,1,0:T(4,128)} %get-tuple-element.418), channel_id=1, source_target_pairs={{0,1},{1,2},{2,3},{4,5},{5,6},{6,7},{8,9},{9,10},{10,11},{12,13},{... | collective-permute-start | bytes 129032 | tf_op jit(solution)/shard_map/ppermute | solution.py:18
  55.3 6.4 %copy-start = (f32[3,14,3,128]{2,1,0,3:T(8,128)S(1)}, f32[3,14,3,128]{2,1,0,3:T(8,128)}, u32[]{:S(2)}) copy-start(f32[3,14,3,128]{2,1,0,3:T(8,128)} %get-tuple-element.414) | copy-start | bytes 193540
  58.5 7.9 %collective-permute-start.4 = (f32[3,14,3,128]{3,1,2,0:T(8,128)}, f32[3,14,3,128]{3,1,2,0:T(8,128)}, u32[]{:S(2)}, u32[]{:S(2)}) collective-permute-start(f32[3,14,3,128]{3,1,2,0:T(8,128)} %copy.49), channel_id=1, source_target_pairs={{1,0},{2,1},{3,2},{5,4},{6,5},{7,6},{9,8},{10,9},{11,10},{13,12},{... | collective-permute-start | bytes 193544 | tf_op jit(solution)/shard_map/ppermute | solution.py:21
  63.5 5.9 %collective-permute-start.3 = (f32[3,14,3,128]{3,1,2,0:T(8,128)}, f32[3,14,3,128]{3,1,2,0:T(8,128)S(1)}, u32[]{:S(2)}, u32[]{:S(2)}) collective-permute-start(f32[3,14,3,128]{3,1,2,0:T(8,128)} %copy.48), channel_id=1, source_target_pairs={{0,1},{1,2},{2,3},{4,5},{5,6},{6,7},{8,9},{9,10},{10,11},{12,13},{... | collective-permute-start | bytes 193544 | tf_op jit(solution)/shard_map/ppermute | solution.py:18
  85.8 3.2 %copy-start.8 = (f32[24,24]{1,0:T(8,128)S(1)}, f32[24,24]{1,0:T(8,128)}, u32[]{:S(2)}) copy-start(f32[24,24]{1,0:T(8,128)} %constant.278.clone.2) | copy-start | bytes 6916 | tf_op jit(solution)/shard_map/cond
  94.5 7.4 %copy-start.7 = (pred[8,16,3]{1,0,2:T(8,128)(4,1)S(1)}, pred[8,16,3]{1,0,2:T(8,128)(4,1)}, u32[]{:S(2)}) copy-start(pred[8,16,3]{1,0,2:T(8,128)(4,1)} %copy-done.6) | copy-start | bytes 1156
  94.5 8.1 %copy-start.1 = (f32[1,3,8,16,128]{3,2,1,4,0:T(8,128)S(1)}, f32[1,3,8,16,128]{3,2,1,4,0:T(8,128)}, u32[]{:S(2)}) copy-start(f32[1,3,8,16,128]{3,2,1,4,0:T(8,128)} %copy.43) | copy-start | bytes 589828
  94.5 8.1 %copy-start.9 = (pred[128]{0:T(512)(128)(4,1)S(1)}, pred[128]{0:T(512)(128)(4,1)}, u32[]{:S(2)}) copy-start(pred[128]{0:T(512)(128)(4,1)} %get-tuple-element.432) | copy-start | bytes 388
  95.7 6.2 %collective-permute-start.13 = (f32[3,8,16,3]{2,1,0,3:T(8,128)}, f32[3,8,16,3]{2,1,0,3:T(8,128)}, u32[]{:S(2)}, u32[]{:S(2)}) collective-permute-start(f32[3,8,16,3]{2,1,0,3:T(8,128)} %slice.2962), channel_id=1, source_target_pairs={{0,16},{1,17},{2,18},{3,19},{4,20},{5,21},{6,22},{7,23},{8,24},{9,... | collective-permute-start | bytes 13832 | tf_op jit(solution)/shard_map/ppermute | solution.py:29
  107.3 2.6 %copy-start.2 = (f32[1,3,8,16,128]{3,2,1,4,0:T(8,128)S(1)}, f32[1,3,8,16,128]{3,2,1,4,0:T(8,128)}, u32[]{:S(2)}) copy-start(f32[1,3,8,16,128]{3,2,1,4,0:T(8,128)} %get-tuple-element.412) | copy-start | bytes 589828
where the time goes:
time: 112 us; the launch traced here: 111 us
  local copies, waits for them, and re-layouts  50.8 us (45%)
  starting transfers between devices  36.3 us (32%)
  other arithmetic  14.4 us (13%)
  waiting for transfers between devices  5.34 us (5%)
  matrix products  2.9 us (3%)
    ppermute x6, starting transfers between devices, with_halo(): lax.ppermute(lax.slice_in_dim(block, block.shape[dim] - width, None, axis...  17.7 us
    cond x25, local copies, waits for them, and re-layouts  16 us
    ppermute x6, starting transfers between devices, with_halo(): lax.ppermute(lax.slice_in_dim(block, 0, width, axis=dim), axis, backward)  15 us
    slice x6, local copies, waits for them, and re-layouts, with_halo(): lax.slice_in_dim(block, block.shape[dim] - width, None, axis=dim)  9.33 us
    unnamed x24, local copies, waits for them, and re-layouts  7.77 us
    slice x3, local copies, waits for them, and re-layouts, with_halo(): lax.slice_in_dim(block, 0, width, axis=dim)  4.85 us
    broadcast_in_dim x1, other arithmetic, per_device(): return (current[None], velocity_now[None])  4.66 us
    concatenate x4, other arithmetic, with_halo(): block = jnp.concatenate([low, block, high], axis=dim)  4.56 us
  transfers between devices with their start and end apart: 14, of which 2 were waited for; matrix products, arithmetic and copies ran while one was open for 28% of the time, Pallas kernels for 0%

commit v1 on v0

--- a/solution.py
+++ b/solution.py
@@ -4,6 +4,8 @@
 import jax.numpy as jnp
 import numpy as np
 from jax import lax
+from jax.experimental import pallas as pl
+from jax.experimental.pallas import tpu as pltpu
 from jax.sharding import PartitionSpec as P
 
 time_step = 0.1
@@ -80,51 +82,76 @@
     return result
 
 
-def bond_sum(field_pad, words_pad, modulus_pad, size_x, size_y, size_z):
-
-    def window(array, delta_x, delta_y, delta_z):
-        return array[
-            ...,
-            3 + delta_x : 3 + delta_x + size_x,
-            3 + delta_y : 3 + delta_y + size_y,
-            3 + delta_z : 3 + delta_z + size_z,
-        ]
-
-    centre = window(field_pad, 0, 0, 0)
-    centre_modulus = window(modulus_pad, 0, 0, 0)
-    centre_words = window(words_pad, 0, 0, 0)
-    summed = jnp.zeros_like(centre)
-    for number, offset in enumerate(half_offsets()):
-        delta_x, delta_y, delta_z = offset
-        word_id = number // 31
-        bit_id = number % 31
-        factor = (
-            0.5
-            * bond_scale
-            / float(delta_x * delta_x + delta_y * delta_y + delta_z * delta_z) ** 1.5
-        )
-        ahead_diff = window(field_pad, delta_x, delta_y, delta_z) - centre
-        behind_diff = window(field_pad, -delta_x, -delta_y, -delta_z) - centre
-        ahead_proj = delta_x * ahead_diff[0] + delta_y * ahead_diff[1] + delta_z * ahead_diff[2]
-        behind_proj = delta_x * behind_diff[0] + delta_y * behind_diff[1] + delta_z * behind_diff[2]
-        ahead_flag = (centre_words[word_id] >> bit_id & 1).astype(jnp.float32)
-        behind_flag = (
-            window(words_pad[word_id], -delta_x, -delta_y, -delta_z) >> bit_id & 1
-        ).astype(jnp.float32)
-        strength = (
-            ahead_flag
-            * (centre_modulus + window(modulus_pad, delta_x, delta_y, delta_z))
-            * ahead_proj
-        )
-        strength = (
-            strength
-            + behind_flag
-            * (centre_modulus + window(modulus_pad, -delta_x, -delta_y, -delta_z))
-            * behind_proj
-        )
-        strength = factor * strength
-        summed = summed + jnp.stack([delta_x * strength, delta_y * strength, delta_z * strength])
-    return summed
+def bond_kernel(values_ref, words_ref, out_ref, values_roll, words_roll):
+    size_x, size_y, depth = out_ref.shape[1:]
+
+    def roll_row(row, carry):
+        for slot in range(7):
+            shift = (3 - slot) % depth
+            for item in range(4):
+                values = values_ref[item, row]
+                values_roll[slot, item, row] = (
+                    pltpu.roll(values, shift, 1) if shift else values
+                )
+            for item in range(2):
+                words = words_ref[item, row]
+                words_roll[slot, item, row] = pltpu.roll(words, shift, 1) if shift else words
+        return carry
+
+    lax.fori_loop(0, values_ref.shape[1], roll_row, 0)
+
+    def one_row(row, carry):
+        rows_y = pl.ds(3, size_y)
+        centre = [values_ref[item, row + 3, rows_y, :] for item in range(4)]
+        centre_words = [words_ref[item, row + 3, rows_y, :] for item in range(2)]
+        sums = [jnp.zeros_like(centre[0]) for _ in range(3)]
+        for number, offset in enumerate(half_offsets()):
+            word_id, bit = number // 31, 1 << (number % 31)
+            factor = 0.5 * bond_scale / float(sum(d * d for d in offset)) ** 1.5
+            for sign in (1, -1):
+                delta = [sign * d for d in offset]
+                slot, place = delta[2] + 3, (row + 3 + delta[0], pl.ds(3 + delta[1], size_y))
+                far = {
+                    item: values_roll[(slot, item) + place]
+                    for item in range(4)
+                    if item == 3 or delta[item]
+                }
+                if sign > 0:
+                    words = centre_words[word_id]
+                else:
+                    words = words_roll[(slot, word_id) + place]
+                projection = None
+                for item in range(3):
+                    if delta[item]:
+                        term = (far[item] - centre[item]) * (factor * delta[item])
+                        projection = term if projection is None else projection + term
+                strength = jnp.where(
+                    (words & bit) != 0, (centre[3] + far[3]) * projection, 0.0
+                )
+                for item in range(3):
+                    if delta[item]:
+                        sums[item] = sums[item] + strength * float(delta[item])
+        for item in range(3):
+            out_ref[item, row] = sums[item]
+        return carry
+
+    lax.fori_loop(0, size_x, one_row, 0)
+
+
+def bond_sum(extended, words_rim, modulus_rim, size_x, size_y, size_z):
+    tail = -extended.shape[2] % 8
+    room = ((0, 0), (0, 0), (0, tail), (0, 0))
+    values = jnp.pad(jnp.concatenate([extended, modulus_rim[None]]), room)
+    words = jnp.pad(words_rim, room)
+    return pl.pallas_call(
+        bond_kernel,
+        out_shape=jax.ShapeDtypeStruct((3, size_x, size_y, size_z), jnp.float32),
+        scratch_shapes=[
+            pltpu.VMEM((7,) + values.shape, jnp.float32),
+            pltpu.VMEM((7,) + words.shape, jnp.int32),
+        ],
+        compiler_params=pltpu.CompilerParams(vmem_limit_bytes=32 * 1024 * 1024),
+    )(values, words)
 
 
 def couple(below_top, map_layers):
@@ -201,9 +228,6 @@
     words_rim = with_halo(bond_words, (("gx", 1), ("gy", 2)), 3)
     modulus_rim = with_halo(modulus[0], (("gx", 0), ("gy", 1)), 3)
     map_layers = jnp.transpose(coupling_map, (1, 2, 0))
-    z_padding = ((0, 0), (0, 0), (0, 0), (3, 3))
-    words_pad = jnp.pad(words_rim, z_padding)
-    modulus_pad = jnp.pad(modulus_rim, ((0, 0), (0, 0), (3, 3)))
     layer_ids = jnp.arange(depth_z)
     moving = (layer_ids >= layers)[None, None, None, :]
     unclamped = (layer_ids > 0)[None, None, None, :]
@@ -223,9 +247,7 @@
     extended = with_halo(current, (("gx", 1), ("gy", 2)), 3)
 
     def zone_branch():
-        return bond_sum(
-            jnp.pad(extended, z_padding), words_pad, modulus_pad, rows_x, rows_y, depth_z
-        )
+        return bond_sum(extended, words_rim, modulus_rim, rows_x, rows_y, depth_z)
 
     def slab_branch():
         return slab_forces(

time: 112 us -> 111 us (level)
  starting transfers between devices: 36.3 us -> 38.6 us
  local copies, waits for them, and re-layouts: 50.8 us -> 48.8 us
  waiting for transfers between devices: 5.34 us -> 3.5 us
    ppermute x6, starting transfers between devices: 15 us -> 18.1 us  [with_halo(): lax.ppermute(lax.slice_in_dim(block, 0, width, axis=dim), axis, backward)]
    ppermute x6, waiting for transfers between devices: 2.1 us -> 0.02 us  [with_halo(): lax.ppermute(lax.slice_in_dim(block, block.shape[dim] - width, None, axis...]
    slice x3, local copies, waits for them, and re-layouts: 4.85 us -> 2.9 us  [with_halo(): lax.slice_in_dim(block, 0, width, axis=dim)]
    ppermute x6, starting transfers between devices: 17.7 us -> 16.2 us  [with_halo(): lax.ppermute(lax.slice_in_dim(block, block.shape[dim] - width, None, axis...]
    concatenate x2, local copies, waits for them, and re-layouts: 2.57 us -> 1.21 us  [with_halo(): block = jnp.concatenate([low, block, high], axis=dim)]
    select_n x1, other arithmetic: 1.37 us -> 0.16 us  [per_device(): jnp.where(is_zone, jnp.concatenate([coupled, current[:, :, :, layers:]],...]
    unnamed x24 -> x28, local copies, waits for them, and re-layouts: 7.77 us -> 7.67 us
    cond x25 -> x27, local copies, waits for them, and re-layouts: 16 us -> 15.9 us
  transfers between devices with their start and end apart: 14 -> 14, of which waited for: 2 -> 2; matrix products, arithmetic and copies ran while one was open for 28% -> 26% of each run, Pallas kernels for 0% -> 0%
where the time goes in v1:
time: 111 us; the launch traced here: 109 us
  local copies, waits for them, and re-layouts  48.8 us (44%)
  starting transfers between devices  38.6 us (35%)
  other arithmetic  14.3 us (13%)
  waiting for transfers between devices  3.5 us (3%)
  matrix products  2.9 us (3%)
    ppermute x6, starting transfers between devices, with_halo(): lax.ppermute(lax.slice_in_dim(block, 0, width, axis=dim), axis, backward)  18.1 us
    ppermute x6, starting transfers between devices, with_halo(): lax.ppermute(lax.slice_in_dim(block, block.shape[dim] - width, None, axis...  16.2 us
    cond x27, local copies, waits for them, and re-layouts  15.9 us
    slice x6, local copies, waits for them, and re-layouts, with_halo(): lax.slice_in_dim(block, block.shape[dim] - width, None, axis=dim)  9.23 us
    unnamed x28, local copies, waits for them, and re-layouts  7.67 us
    broadcast_in_dim x1, other arithmetic, per_device(): return (current[None], velocity_now[None])  4.69 us
    concatenate x4, other arithmetic, with_halo(): block = jnp.concatenate([low, block, high], axis=dim)  4.36 us
    ppermute x2, starting transfers between devices, passed_along(): return lax.ppermute(block, axis, route)  4.3 us
  transfers between devices with their start and end apart: 14, of which 2 were waited for; matrix products, arithmetic and copies ran while one was open for 26% of the time, Pallas kernels for 0%

profile of v1, /device:TPU:14, one launch (start us, length us, event | category | flops | bytes accessed | tf_op | source)
XLA Modules:
  0.0 109.3 jit_solution(10279913417813483393)
XLA Ops:
  2.8 3.0 %collective-permute-start = (f32[3,8,16,3]{2,1,0,3:T(8,128)}, f32[3,8,16,3]{2,1,0,3:T(8,128)}, u32[]{:S(2)}, u32[]{:S(2)}) collective-permute-start(f32[3,8,16,3]{2,1,0,3:T(8,128)} %slice.312), channel_id=1, source_target_pairs={{16,0},{17,1},{18,2},{19,3},{20,4},{21,5},{22,6},{23,7},{24,8},{25... | collective-permute-start | bytes 13832 | tf_op jit(solution)/shard_map/ppermute | solution.py:31
  7.2 3.5 %collective-permute-start.5 = (f32[3,16,128]{2,1,0:T(8,128)}, f32[3,16,128]{2,1,0:T(8,128)S(1)}, u32[]{:S(2)}, u32[]{:S(2)}) collective-permute-start(f32[3,16,128]{2,1,0:T(8,128)} %get-tuple-element.70), channel_id=1, source_target_pairs={{0,4},{4,8},{8,12},{1,5},{5,9},{9,13},{2,6},{6,10},{10,14},{3,7},{... | collective-permute-start | bytes 73736 | tf_op jit(solution)/shard_map/ppermute | solution.py:20
  10.6 2.4 %collective-permute-start.6 = (f32[3,16,128]{2,1,0:T(8,128)}, f32[3,16,128]{2,1,0:T(8,128)S(1)}, u32[]{:S(2)}, u32[]{:S(2)}) collective-permute-start(f32[3,16,128]{2,1,0:T(8,128)} %get-tuple-element.71), channel_id=1, source_target_pairs={{4,0},{8,4},{12,8},{5,1},{9,5},{13,9},{6,2},{10,6},{14,10},{7,3},{... | collective-permute-start | bytes 73736 | tf_op jit(solution)/shard_map/ppermute | solution.py:23
  13.8 3.5 %collective-permute-start.9 = (s32[2,3,16,128]{3,2,1,0:T(8,128)S(1)}, s32[2,3,16,128]{3,2,1,0:T(8,128)S(1)}, u32[]{:S(2)}, u32[]{:S(2)}) collective-permute-start(s32[2,3,16,128]{3,2,1,0:T(8,128)S(1)} %get-tuple-element.67), channel_id=1, source_target_pairs={{0,4},{4,8},{8,12},{1,5},{5,9},{9,13},{2,6},{6,10},{10,14},{3,7},{... | collective-permute-start | bytes 147464 | tf_op jit(solution)/shard_map/ppermute | solution.py:20
  17.3 2.4 %collective-permute-start.10 = (s32[2,3,16,128]{3,2,1,0:T(8,128)S(1)}, s32[2,3,16,128]{3,2,1,0:T(8,128)S(1)}, u32[]{:S(2)}, u32[]{:S(2)}) collective-permute-start(s32[2,3,16,128]{3,2,1,0:T(8,128)S(1)} %get-tuple-element.66), channel_id=1, source_target_pairs={{4,0},{8,4},{12,8},{5,1},{9,5},{13,9},{6,2},{10,6},{14,10},{7,3},{... | collective-permute-start | bytes 147464 | tf_op jit(solution)/shard_map/ppermute | solution.py:23
  26.1 1.9 %collective-permute-start.7 = (f32[14,3,128]{2,1,0:T(4,128)S(1)}, f32[14,3,128]{2,1,0:T(4,128)S(1)}, u32[]{:S(2)}, u32[]{:S(2)}) collective-permute-start(f32[14,3,128]{2,1,0:T(4,128)S(1)} %get-tuple-element.68), channel_id=1, source_target_pairs={{0,1},{1,2},{2,3},{4,5},{5,6},{6,7},{8,9},{9,10},{10,11},{12,13},{... | collective-permute-start | bytes 64520 | tf_op jit(solution)/shard_map/ppermute | solution.py:20
  28.0 3.8 %collective-permute-start.8 = (f32[14,3,128]{2,1,0:T(4,128)S(1)}, f32[14,3,128]{2,1,0:T(4,128)S(1)}, u32[]{:S(2)}, u32[]{:S(2)}) collective-permute-start(f32[14,3,128]{2,1,0:T(4,128)S(1)} %get-tuple-element.69), channel_id=1, source_target_pairs={{1,0},{2,1},{3,2},{5,4},{6,5},{7,6},{9,8},{10,9},{11,10},{13,12},{... | collective-permute-start | bytes 64520 | tf_op jit(solution)/shard_map/ppermute | solution.py:23
  32.3 3.5 %collective-permute-start.1 = (f32[3,3,16,128]{3,2,1,0:T(8,128)S(1)}, f32[3,3,16,128]{3,2,1,0:T(8,128)S(1)}, u32[]{:S(2)}, u32[]{:S(2)}) collective-permute-start(f32[3,3,16,128]{3,2,1,0:T(8,128)S(1)} %copy.44), channel_id=1, source_target_pairs={{0,4},{4,8},{8,12},{1,5},{5,9},{9,13},{2,6},{6,10},{10,14},{3,7},{... | collective-permute-start | bytes 221192 | tf_op jit(solution)/shard_map/ppermute | solution.py:20
  36.1 2.4 %collective-permute-start.2 = (f32[3,3,16,128]{3,2,1,0:T(8,128)S(1)}, f32[3,3,16,128]{3,2,1,0:T(8,128)S(1)}, u32[]{:S(2)}, u32[]{:S(2)}) collective-permute-start(f32[3,3,16,128]{3,2,1,0:T(8,128)S(1)} %copy.45), channel_id=1, source_target_pairs={{4,0},{8,4},{12,8},{5,1},{9,5},{13,9},{6,2},{10,6},{14,10},{7,3},{... | collective-permute-start | bytes 221192 | tf_op jit(solution)/shard_map/ppermute | solution.py:23
  40.6 1.9 %collective-permute-start.11 = (s32[2,14,3,128]{3,2,1,0:T(4,128)}, s32[2,14,3,128]{3,2,1,0:T(4,128)}, u32[]{:S(2)}, u32[]{:S(2)}) collective-permute-start(s32[2,14,3,128]{3,2,1,0:T(4,128)} %get-tuple-element.64), channel_id=1, source_target_pairs={{0,1},{1,2},{2,3},{4,5},{5,6},{6,7},{8,9},{9,10},{10,11},{12,13},{... | collective-permute-start | bytes 129032 | tf_op jit(solution)/shard_map/ppermute | solution.py:20
  42.5 3.6 %collective-permute-start.12 = (s32[2,14,3,128]{3,2,1,0:T(4,128)S(1)}, s32[2,14,3,128]{3,2,1,0:T(4,128)}, u32[]{:S(2)}, u32[]{:S(2)}) collective-permute-start(s32[2,14,3,128]{3,2,1,0:T(4,128)S(1)} %get-tuple-element.65), channel_id=1, source_target_pairs={{1,0},{2,1},{3,2},{5,4},{6,5},{7,6},{9,8},{10,9},{11,10},{13,12},{... | collective-permute-start | bytes 129032 | tf_op jit(solution)/shard_map/ppermute | solution.py:23
  48.5 2.6 %pad_maximum_fusion.1 = f32[3,14,16,128]{2,1,0,3:T(8,128)S(1)} fusion(f32[3,3,16,128]{2,1,0,3:T(4,128)} %copy.47, f32[3,8,16,128]{2,1,0,3:T(8,128)} %copy-done, f32[3,3,16,128]{2,1,0,3:T(4,128)} %copy.46), kind=kLoop, calls=%fused_computation.81 | loop fusion | flops 172032 | bytes 688128 | tf_op jit(solution)/shard_map/concatenate | solution.py:24
  51.1 3.6 %fusion.43 = (f32[3,14,3,128]{2,1,0,3:T(8,128)}, f32[3,14,3,128]{2,1,0,3:T(8,128)}) fusion(f32[3,14,16,128]{2,1,0,3:T(8,128)S(1)} %pad_maximum_fusion.1), kind=kLoop, calls=%fused_computation.130 | loop fusion | bytes 258048 | tf_op jit(solution)/shard_map/slice | solution.py:21
  55.9 3.1 %copy.48 = f32[3,14,3,128]{3,1,2,0:T(8,128)} copy(f32[3,14,3,128]{2,1,0,3:T(8,128)} %get-tuple-element.60) | data formatting | bytes 129024 | tf_op jit(solution)/shard_map/slice | solution.py:21
  59.0 1.9 %collective-permute-start.3 = (f32[3,14,3,128]{3,1,2,0:T(8,128)}, f32[3,14,3,128]{3,1,2,0:T(8,128)}, u32[]{:S(2)}, u32[]{:S(2)}) collective-permute-start(f32[3,14,3,128]{3,1,2,0:T(8,128)} %copy.48), channel_id=1, source_target_pairs={{0,1},{1,2},{2,3},{4,5},{5,6},{6,7},{8,9},{9,10},{10,11},{12,13},{... | collective-permute-start | bytes 193544 | tf_op jit(solution)/shard_map/ppermute | solution.py:20
  61.0 1.8 %copy.49 = f32[3,14,3,128]{3,1,2,0:T(8,128)} copy(f32[3,14,3,128]{2,1,0,3:T(8,128)S(1)} %copy-done.2) | data formatting | bytes 129024 | tf_op jit(solution)/shard_map/slice | solution.py:23
  62.8 3.6 %collective-permute-start.4 = (f32[3,14,3,128]{3,1,2,0:T(8,128)}, f32[3,14,3,128]{3,1,2,0:T(8,128)S(1)}, u32[]{:S(2)}, u32[]{:S(2)}) collective-permute-start(f32[3,14,3,128]{3,1,2,0:T(8,128)} %copy.49), channel_id=1, source_target_pairs={{1,0},{2,1},{3,2},{5,4},{6,5},{7,6},{9,8},{10,9},{11,10},{13,12},{... | collective-permute-start | bytes 193544 | tf_op jit(solution)/shard_map/ppermute | solution.py:23
  68.8 23.8 %conditional.1 = (f32[3,8,16,128]{3,2,1,0:T(8,128)S(1)}) conditional(s32[]{:T(128)} %convert_element_type.54, (f32[3,14,22,128]{3,2,1,0:T(8,128)S(1)}, s32[]{:T(128)}, s32[]{:T(128)}, f32[14,22,128]{2,1,0:T(8,128)}) %tuple.18, (f32[14,22,128]{2,1,0:T(8,128)}, f32[3,14,22,128]{3,2,1,0:T(8,128)S(1)}, s32[2,14,22,128]{3,2,1,0:T(8,128)S(1)}) %tuple.15), branch_computations={%region_0.1_spmd.clone, %region_1.2_spmd} | conditional | flops 136365696 | bytes 29220292 | solution.py:257
  85.5 1.8 %reshape.138 = f32[24,19584]{1,0:T(8,128)S(1)} reshape(f32[24,9,17,128]{3,2,1,0:T(8,128)} %fusion.11) | data formatting | bytes 3760128 | tf_op jit(solution)/shard_map/cond/branch_0_fun/reshape | solution.py:188
  87.4 2.9 %fusion.47 = f32[24,19584]{1,0:T(8,128)} fusion(f32[24,24]{1,0:T(8,128)S(1)} %copy-done.11, f32[24,19584]{1,0:T(8,128)S(1)} %reshape.138), kind=kOutput, calls=%fused_computation.134 | convolution fusion | flops 135364608 | bytes 3762432 | tf_op jit(solution)/shard_map/cond/branch_0_fun/dot_general | solution.py:197
  95.2 1.7 %copy.54 = f32[3,8,16,128]{2,1,0,3:T(8,128)} copy(f32[3,8,16,128]{3,2,1,0:T(8,128)S(1)} %broadcast_multiply_fusion.1) | data formatting | bytes 393216 | tf_op jit(solution)/shard_map/mul | solution.py:263
  96.8 3.2 %collective-permute-done.13 = f32[3,8,16,3]{2,1,0,3:T(8,128)} collective-permute-done((f32[3,8,16,3]{2,1,0,3:T(8,128)}, f32[3,8,16,3]{2,1,0,3:T(8,128)}, u32[]{:S(2)}, u32[]{:S(2)}) %collective-permute-start.13) | collective-permute-done | bytes 4640 | tf_op jit(solution)/shard_map/ppermute | solution.py:31
  100.8 4.7 %select_bitcast_fusion = (f32[1,3,8,16,128]{3,2,1,4,0:T(8,128)}, f32[1,3,8,16,128]{3,2,1,4,0:T(8,128)}) fusion(pred[]{:T(512)S(6)} %eq.27, f32[3,8,16,128]{2,1,0,3:T(8,128)} %copy.54, f32[1,3,8,16,128]{3,2,1,4,0:T(8,128)} %copy.43, pred[128]{0:T(512)(128)(4,1)} %get-tuple-element.79, f32[8,16,128]{1,0,2:T(8,128)} %multiply_multiply_fusion, ...), kind=kLoop, calls=%fused_computation.95 | loop fusion | flops 1032192 | bytes 1250049 | tf_op jit(solution)/shard_map/broadcast_in_dim | solution.py:269
  105.5 2.6 %copy.57 = f32[1,3,8,16,128]{4,3,2,1,0:T(8,128)} copy(f32[1,3,8,16,128]{3,2,1,4,0:T(8,128)} %get-tuple-element.59) | data formatting | bytes 393216
  (110 shorter events, 42.9 us)
Async XLA Ops:
  0.6 22.1 %copy-start.8 = (f32[1,3,8,16,128]{4,3,2,1,0:T(8,128)S(1)}, f32[1,3,8,16,128]{4,3,2,1,0:T(8,128)}, u32[]{:S(2)}) copy-start(f32[1,3,8,16,128]{4,3,2,1,0:T(8,128)} %param.9) | copy-start | bytes 589828
  2.8 21.6 %collective-permute-start = (f32[3,8,16,3]{2,1,0,3:T(8,128)}, f32[3,8,16,3]{2,1,0,3:T(8,128)}, u32[]{:S(2)}, u32[]{:S(2)}) collective-permute-start(f32[3,8,16,3]{2,1,0,3:T(8,128)} %slice.312), channel_id=1, source_target_pairs={{16,0},{17,1},{18,2},{19,3},{20,4},{21,5},{22,6},{23,7},{24,8},{25... | collective-permute-start | bytes 13832 | tf_op jit(solution)/shard_map/ppermute | solution.py:31
  7.2 18.9 %collective-permute-start.5 = (f32[3,16,128]{2,1,0:T(8,128)}, f32[3,16,128]{2,1,0:T(8,128)S(1)}, u32[]{:S(2)}, u32[]{:S(2)}) collective-permute-start(f32[3,16,128]{2,1,0:T(8,128)} %get-tuple-element.70), channel_id=1, source_target_pairs={{0,4},{4,8},{8,12},{1,5},{5,9},{9,13},{2,6},{6,10},{10,14},{3,7},{... | collective-permute-start | bytes 73736 | tf_op jit(solution)/shard_map/ppermute | solution.py:20
  10.6 15.4 %collective-permute-start.6 = (f32[3,16,128]{2,1,0:T(8,128)}, f32[3,16,128]{2,1,0:T(8,128)S(1)}, u32[]{:S(2)}, u32[]{:S(2)}) collective-permute-start(f32[3,16,128]{2,1,0:T(8,128)} %get-tuple-element.71), channel_id=1, source_target_pairs={{4,0},{8,4},{12,8},{5,1},{9,5},{13,9},{6,2},{10,6},{14,10},{7,3},{... | collective-permute-start | bytes 73736 | tf_op jit(solution)/shard_map/ppermute | solution.py:23
  13.8 25.3 %collective-permute-start.9 = (s32[2,3,16,128]{3,2,1,0:T(8,128)S(1)}, s32[2,3,16,128]{3,2,1,0:T(8,128)S(1)}, u32[]{:S(2)}, u32[]{:S(2)}) collective-permute-start(s32[2,3,16,128]{3,2,1,0:T(8,128)S(1)} %get-tuple-element.67), channel_id=1, source_target_pairs={{0,4},{4,8},{8,12},{1,5},{5,9},{9,13},{2,6},{6,10},{10,14},{3,7},{... | collective-permute-start | bytes 147464 | tf_op jit(solution)/shard_map/ppermute | solution.py:20
  17.3 21.9 %collective-permute-start.10 = (s32[2,3,16,128]{3,2,1,0:T(8,128)S(1)}, s32[2,3,16,128]{3,2,1,0:T(8,128)S(1)}, u32[]{:S(2)}, u32[]{:S(2)}) collective-permute-start(s32[2,3,16,128]{3,2,1,0:T(8,128)S(1)} %get-tuple-element.66), channel_id=1, source_target_pairs={{4,0},{8,4},{12,8},{5,1},{9,5},{13,9},{6,2},{10,6},{14,10},{7,3},{... | collective-permute-start | bytes 147464 | tf_op jit(solution)/shard_map/ppermute | solution.py:23
  26.0 5.8 %copy-start = (f32[3,8,16,128]{2,1,0,3:T(8,128)}, f32[3,8,16,128]{2,1,0,3:T(8,128)S(1)}, u32[]{:S(2)}) copy-start(f32[3,8,16,128]{2,1,0,3:T(8,128)S(1)} %maximum_select_fusion) | copy-start | bytes 589828
  26.1 10.0 %collective-permute-start.7 = (f32[14,3,128]{2,1,0:T(4,128)S(1)}, f32[14,3,128]{2,1,0:T(4,128)S(1)}, u32[]{:S(2)}, u32[]{:S(2)}) collective-permute-start(f32[14,3,128]{2,1,0:T(4,128)S(1)} %get-tuple-element.68), channel_id=1, source_target_pairs={{0,1},{1,2},{2,3},{4,5},{5,6},{6,7},{8,9},{9,10},{10,11},{12,13},{... | collective-permute-start | bytes 64520 | tf_op jit(solution)/shard_map/ppermute | solution.py:20
  28.0 11.2 %copy-start.7 = (s32[2,8,16,128]{3,2,1,0:T(8,128)S(1)}, s32[2,8,16,128]{3,2,1,0:T(8,128)}, u32[]{:S(2)}) copy-start(s32[2,8,16,128]{3,2,1,0:T(8,128)} %param.11) | copy-start | bytes 393220
  28.0 10.4 %collective-permute-start.8 = (f32[14,3,128]{2,1,0:T(4,128)S(1)}, f32[14,3,128]{2,1,0:T(4,128)S(1)}, u32[]{:S(2)}, u32[]{:S(2)}) collective-permute-start(f32[14,3,128]{2,1,0:T(4,128)S(1)} %get-tuple-element.69), channel_id=1, source_target_pairs={{1,0},{2,1},{3,2},{5,4},{6,5},{7,6},{9,8},{10,9},{11,10},{13,12},{... | collective-permute-start | bytes 64520 | tf_op jit(solution)/shard_map/ppermute | solution.py:23
  32.3 13.8 %collective-permute-start.1 = (f32[3,3,16,128]{3,2,1,0:T(8,128)S(1)}, f32[3,3,16,128]{3,2,1,0:T(8,128)S(1)}, u32[]{:S(2)}, u32[]{:S(2)}) collective-permute-start(f32[3,3,16,128]{3,2,1,0:T(8,128)S(1)} %copy.44), channel_id=1, source_target_pairs={{0,4},{4,8},{8,12},{1,5},{5,9},{9,13},{2,6},{6,10},{10,14},{3,7},{... | collective-permute-start | bytes 221192 | tf_op jit(solution)/shard_map/ppermute | solution.py:20
  36.1 11.3 %collective-permute-start.2 = (f32[3,3,16,128]{3,2,1,0:T(8,128)S(1)}, f32[3,3,16,128]{3,2,1,0:T(8,128)S(1)}, u32[]{:S(2)}, u32[]{:S(2)}) collective-permute-start(f32[3,3,16,128]{3,2,1,0:T(8,128)S(1)} %copy.45), channel_id=1, source_target_pairs={{4,0},{8,4},{12,8},{5,1},{9,5},{13,9},{6,2},{10,6},{14,10},{7,3},{... | collective-permute-start | bytes 221192 | tf_op jit(solution)/shard_map/ppermute | solution.py:23
  40.6 25.8 %collective-permute-start.11 = (s32[2,14,3,128]{3,2,1,0:T(4,128)}, s32[2,14,3,128]{3,2,1,0:T(4,128)}, u32[]{:S(2)}, u32[]{:S(2)}) collective-permute-start(s32[2,14,3,128]{3,2,1,0:T(4,128)} %get-tuple-element.64), channel_id=1, source_target_pairs={{0,1},{1,2},{2,3},{4,5},{5,6},{6,7},{8,9},{9,10},{10,11},{12,13},{... | collective-permute-start | bytes 129032 | tf_op jit(solution)/shard_map/ppermute | solution.py:20
  42.5 23.9 %collective-permute-start.12 = (s32[2,14,3,128]{3,2,1,0:T(4,128)S(1)}, s32[2,14,3,128]{3,2,1,0:T(4,128)}, u32[]{:S(2)}, u32[]{:S(2)}) collective-permute-start(s32[2,14,3,128]{3,2,1,0:T(4,128)S(1)} %get-tuple-element.65), channel_id=1, source_target_pairs={{1,0},{2,1},{3,2},{5,4},{6,5},{7,6},{9,8},{10,9},{11,10},{13,12},{... | collective-permute-start | bytes 129032 | tf_op jit(solution)/shard_map/ppermute | solution.py:23
  55.9 5.1 %copy-start.2 = (f32[3,14,3,128]{2,1,0,3:T(8,128)S(1)}, f32[3,14,3,128]{2,1,0,3:T(8,128)}, u32[]{:S(2)}) copy-start(f32[3,14,3,128]{2,1,0,3:T(8,128)} %get-tuple-element.61) | copy-start | bytes 193540
  59.0 8.4 %collective-permute-start.3 = (f32[3,14,3,128]{3,1,2,0:T(8,128)}, f32[3,14,3,128]{3,1,2,0:T(8,128)}, u32[]{:S(2)}, u32[]{:S(2)}) collective-permute-start(f32[3,14,3,128]{3,1,2,0:T(8,128)} %copy.48), channel_id=1, source_target_pairs={{0,1},{1,2},{2,3},{4,5},{5,6},{6,7},{8,9},{9,10},{10,11},{12,13},{... | collective-permute-start | bytes 193544 | tf_op jit(solution)/shard_map/ppermute | solution.py:20
  62.8 5.9 %collective-permute-start.4 = (f32[3,14,3,128]{3,1,2,0:T(8,128)}, f32[3,14,3,128]{3,1,2,0:T(8,128)S(1)}, u32[]{:S(2)}, u32[]{:S(2)}) collective-permute-start(f32[3,14,3,128]{3,1,2,0:T(8,128)} %copy.49), channel_id=1, source_target_pairs={{1,0},{2,1},{3,2},{5,4},{6,5},{7,6},{9,8},{10,9},{11,10},{13,12},{... | collective-permute-start | bytes 193544 | tf_op jit(solution)/shard_map/ppermute | solution.py:23
  84.1 3.2 %copy-start.11 = (f32[24,24]{1,0:T(8,128)S(1)}, f32[24,24]{1,0:T(8,128)}, u32[]{:S(2)}) copy-start(f32[24,24]{1,0:T(8,128)} %constant.67.clone.2) | copy-start | bytes 6916 | tf_op jit(solution)/shard_map/cond
  92.6 7.4 %copy-start.9 = (pred[8,16,3]{1,0,2:T(8,128)(4,1)S(1)}, pred[8,16,3]{1,0,2:T(8,128)(4,1)}, u32[]{:S(2)}) copy-start(pred[8,16,3]{1,0,2:T(8,128)(4,1)} %get-tuple-element.76) | copy-start | bytes 1156
  92.7 7.4 %copy-start.10 = (pred[8,16,3]{1,0,2:T(8,128)(4,1)S(1)}, pred[8,16,3]{1,0,2:T(8,128)(4,1)}, u32[]{:S(2)}) copy-start(pred[8,16,3]{1,0,2:T(8,128)(4,1)} %get-tuple-element.77) | copy-start | bytes 1156
  92.7 8.1 %copy-start.1 = (f32[3,8,16,128]{2,1,0,3:T(8,128)S(1)}, f32[3,8,16,128]{2,1,0,3:T(8,128)}, u32[]{:S(2)}) copy-start(f32[3,8,16,128]{2,1,0,3:T(8,128)} %copy-done) | copy-start | bytes 589828
  92.7 8.1 %copy-start.12 = (pred[128]{0:T(512)(128)(4,1)S(1)}, pred[128]{0:T(512)(128)(4,1)}, u32[]{:S(2)}) copy-start(pred[128]{0:T(512)(128)(4,1)} %get-tuple-element.78) | copy-start | bytes 388
  93.9 6.2 %collective-permute-start.13 = (f32[3,8,16,3]{2,1,0,3:T(8,128)}, f32[3,8,16,3]{2,1,0,3:T(8,128)}, u32[]{:S(2)}, u32[]{:S(2)}) collective-permute-start(f32[3,8,16,3]{2,1,0,3:T(8,128)} %slice.323), channel_id=1, source_target_pairs={{0,16},{1,17},{2,18},{3,19},{4,20},{5,21},{6,22},{7,23},{8,24},{9,... | collective-permute-start | bytes 13832 | tf_op jit(solution)/shard_map/ppermute | solution.py:31
  105.5 2.6 %copy-start.3 = (f32[1,3,8,16,128]{3,2,1,4,0:T(8,128)S(1)}, f32[1,3,8,16,128]{3,2,1,4,0:T(8,128)}, u32[]{:S(2)}) copy-start(f32[1,3,8,16,128]{3,2,1,4,0:T(8,128)} %get-tuple-element.58) | copy-start | bytes 589828
  (3 other events, 4.2 us)
